TPU v7x, 32 devices: a whole 2x2x4 slice. The times are simulated.
32 devices in a mesh: rows: 16 (over z, x, core), cols: 2 (over y).
Axes of the slice: x: 2, y: 2, z: 4, core: 2. Of those that a mesh axis runs over, the one named last changes fastest.
Arguments:
- kernel: float32 [16384, 1536], P('rows', 'cols'), may hold values from -0.15625 to 0.15625
- row_orbitals: float32 [16384, 512], P('rows', 'cols'), may hold values from -1.5 to 1.5
- col_orbitals: float32 [1536, 512], P('cols', 'rows'), may hold values from -1.5 to 1.5
- col_vectors: float32 [1536, 512], P('cols', 'rows'), may hold values from -6 to 6
Outputs:
- exchange: float32 [512, 16384], P('cols', 'rows')
All inputs are finite; a program needn't handle non-finite values.
Results may differ from a plain program's by a relative error of at most 0.0003.
Values sent between devices are 32-bit elements; how exact they have to be, the bound alone decides.
A program may use at most 64 MiB of HBM per device.

v0:
```python
import jax
import jax.numpy as jnp
from jax import lax
from jax.sharding import PartitionSpec as P


def body(kernel, row_orbitals, col_orbitals, col_vectors):
    full_rows = lax.all_gather(row_orbitals, "cols", axis=1, tiled=True)
    full_cols = lax.all_gather(col_orbitals, "rows", axis=1, tiled=True)
    full_vecs = lax.all_gather(col_vectors, "rows", axis=1, tiled=True)
    gram = jnp.dot(
        full_rows, full_cols.T, precision=lax.Precision.HIGHEST, preferred_element_type=jnp.float32
    )
    weighted = kernel * gram
    return lax.psum_scatter(
        -jnp.dot(
            full_vecs.T,
            weighted.T,
            precision=lax.Precision.HIGHEST,
            preferred_element_type=jnp.float32,
        ),
        "cols",
        scatter_dimension=0,
        tiled=True,
    )


def solution(mesh):
    in_specs = (P("rows", "cols"), P("rows", "cols"), P("cols", "rows"), P("cols", "rows"))
    out_specs = P("cols", "rows")
    return jax.shard_map(body, mesh=mesh, in_specs=in_specs, out_specs=out_specs, check_vma=False)
```

profile of v0, /device:TPU:0, one launch (start us, length us, event | category | flops | bytes accessed | tf_op | source)
XLA Modules:
  0.0 175.4 jit_solution(11052527146017626073)
XLA Ops:
  6.5 0.0 all-gather.4.cloned.1.call-start
  6.5 0.7 all-gather.4.cloned.1.call-update
  7.3 0.0 all-gather.6.cloned.1.call-start
  7.3 0.7 all-gather.6.cloned.1.call-update
  8.0 0.0 all-gather.8.cloned.1.call-start
  8.1 0.7 all-gather.8.cloned.1.call-update
  8.7 0.0 reduce-scatter.2.cloned.1.call-start
  8.8 35.9 %all-gather.4.cloned.1.call-done = f32[1024,512]{1,0:T(8,128)} async-done(((f32[1024,256]{1,0:T(8,128)}), f32[1024,512]{1,0:T(8,128)}) %all-gather.4.cloned.1.call-update) | async-done | bytes 2097168 | tf_op jit(solution)/shard_map/all_gather | solution.py:8
  44.7 41.9 %all-gather.6.cloned.1.call-done = f32[768,512]{0,1:T(8,128)} async-done(((f32[768,32]{0,1:T(8,128)}), f32[768,512]{0,1:T(8,128)}) %all-gather.6.cloned.1.call-update) | async-done | bytes 1572880 | tf_op jit(solution)/shard_map/all_gather | solution.py:9
  86.6 7.2 %fusion.4 = f32[1024,768]{1,0:T(8,128)S(1)} fusion(f32[1024,512]{1,0:T(8,128)} %all-gather.4.cloned.1.call-done, f32[768,512]{0,1:T(8,128)} %all-gather.6.cloned.1.call-done), kind=kOutput, calls=%fused_computation.3 | convolution fusion | flops 4831838208 | bytes 6815744 | tf_op jit(solution)/shard_map/dot_general | solution.py:11
  93.9 33.4 %all-gather.8.cloned.1.call-done = f32[768,512]{0,1:T(8,128)} async-done(((f32[768,32]{0,1:T(8,128)}), f32[768,512]{0,1:T(8,128)}) %all-gather.8.cloned.1.call-update) | async-done | bytes 1572880 | tf_op jit(solution)/shard_map/all_gather | solution.py:10
  127.3 8.3 %negate_bitcast_fusion = f32[512,1024]{0,1:T(8,128)} fusion(f32[768,512]{0,1:T(8,128)} %all-gather.8.cloned.1.call-done, f32[1024,768]{1,0:T(8,128)} %param.4, f32[1024,768]{1,0:T(8,128)S(1)} %fusion.4), kind=kOutput, calls=%fused_computation.2 | convolution fusion | flops 4833148928 | bytes 9961472 | tf_op jit(solution)/shard_map/dot_general | solution.py:16
  135.6 0.0 reduce-scatter.2.cloned.1.call-update
  135.6 30.8 %reduce-scatter.2.cloned.1.call-done = f32[256,1024]{0,1:T(8,128)} async-done(((f32[512,1024]{0,1:T(8,128)}), f32[256,1024]{0,1:T(8,128)}) %reduce-scatter.2.cloned.1.call-update) | async-done | bytes 1048592 | tf_op jit(solution)/shard_map/reduce_scatter | solution.py:15
  166.4 2.5 %copy.5 = f32[256,1024]{1,0:T(8,128)} copy(f32[256,1024]{0,1:T(8,128)} %reduce-scatter.2.cloned.1.call-done) | data formatting | bytes 2097152 | tf_op jit(solution)/shard_map/reduce_scatter | solution.py:15
Async XLA Ops:
  6.5 38.2 %all-gather.4.cloned.1.call-start = ((), (), s32[]{:S(2)}) async-start(), calls=%async_computation.1 | async-start | bytes 3145728 | tf_op jit(solution)/shard_map/all_gather | solution.py:8
  7.3 79.4 %all-gather.6.cloned.1.call-start = ((), (), s32[]{:S(2)}) async-start(), calls=%async_computation.2 | async-start | bytes 1671168 | tf_op jit(solution)/shard_map/all_gather | solution.py:9
  8.0 119.3 %all-gather.8.cloned.1.call-start = ((), (), s32[]{:S(2)}) async-start(), calls=%async_computation.3 | async-start | bytes 1671168 | tf_op jit(solution)/shard_map/all_gather | solution.py:10
  8.7 157.6 %reduce-scatter.2.cloned.1.call-start = ((), (), s32[]{:S(2)}) async-start(), calls=%async_computation.4 | async-start | bytes 3145728 | tf_op jit(solution)/shard_map/reduce_scatter | solution.py:15
Sparse Core Ops, SparseCore 0:
  8.9 35.8 all-gather.3
  47.0 39.5 all-gather.5
  88.9 38.2 all-gather.7
  135.7 30.6 reduce-scatter.1
where the time goes:
time: 176 us; the launch traced here: 175 us
  waiting for transfers between devices  144 us (82%)
  matrix products  15.6 us (9%)
  between operations  13.1 us (7%)
  local copies, waits for them, and re-layouts  2.53 us (1%)
    all_gather x1, waiting for transfers between devices, body(): full_cols = lax.all_gather(col_orbitals, 'rows', axis=1, tiled=True)  41.9 us
    all_gather x1, waiting for transfers between devices, body(): full_rows = lax.all_gather(row_orbitals, 'cols', axis=1, tiled=True)  35.9 us
    all_gather x1, waiting for transfers between devices, body(): full_vecs = lax.all_gather(col_vectors, 'rows', axis=1, tiled=True)  33.4 us
    reduce_scatter x1, waiting for transfers between devices, body(): lax.psum_scatter(-jnp.dot(full_vecs.T, weighted.T, precision=lax.Precisio...  30.8 us
    dot_general x1, matrix products, body(): jnp.dot(full_vecs.T, weighted.T, precision=lax.Precision.HIGHEST, preferr...  8.31 us
    dot_general x1, matrix products, body(): jnp.dot(full_rows, full_cols.T, precision=lax.Precision.HIGHEST, preferre...  7.25 us
  transfers between devices with their start and end apart: 4, of which 4 were waited for; matrix products, arithmetic and copies ran while one was open for 4% of the time, Pallas kernels for 0%

commit v1 on v0

--- a/solution.py
+++ b/solution.py
@@ -7,7 +7,7 @@
 def body(kernel, row_orbitals, col_orbitals, col_vectors):
     full_rows = lax.all_gather(row_orbitals, "cols", axis=1, tiled=True)
     full_cols = lax.all_gather(col_orbitals, "rows", axis=1, tiled=True)
-    full_vecs = lax.all_gather(col_vectors, "rows", axis=1, tiled=True)
+    full_vecs = jnp.concatenate(lax.all_gather(col_vectors, "rows"), axis=1)
     gram = jnp.dot(
         full_rows, full_cols.T, precision=lax.Precision.HIGHEST, preferred_element_type=jnp.float32
     )

time: 176 us -> 182 us (1.034)
  waiting for transfers between devices: 144 us -> 149 us
  local copies, waits for them, and re-layouts: 2.53 us -> 5.34 us
    all_gather x1, waiting for transfers between devices: 33.4 us -> 43.2 us  [body(): full_vecs = jnp.concatenate(lax.all_gather(col_vectors, 'rows'), axis=1)]
    all_gather x1, waiting for transfers between devices: 35.9 us -> 30.6 us  [body(): full_rows = lax.all_gather(row_orbitals, 'cols', axis=1, tiled=True)]
    unnamed x0 -> x3, local copies, waits for them, and re-layouts: none -> 1.89 us
    dot_general x1, matrix products: 8.31 us -> 6.46 us  [body(): jnp.dot(full_vecs.T, weighted.T, precision=lax.Precision.HIGHEST, preferr...]
  transfers between devices with their start and end apart: 4 -> 4, of which waited for: 4 -> 4; matrix products, arithmetic and copies ran while one was open for 4% -> 2% of each run, Pallas kernels for 0% -> 0%
where the time goes in v1:
time: 182 us; the launch traced here: 181 us
  waiting for transfers between devices  149 us (82%)
  matrix products  14.2 us (8%)
  between operations  13.2 us (7%)
  local copies, waits for them, and re-layouts  5.34 us (3%)
    all_gather x1, waiting for transfers between devices, body(): full_vecs = jnp.concatenate(lax.all_gather(col_vectors, 'rows'), axis=1)  43.2 us
    all_gather x1, waiting for transfers between devices, body(): full_cols = lax.all_gather(col_orbitals, 'rows', axis=1, tiled=True)  41.9 us
    reduce_scatter x1, waiting for transfers between devices, body(): lax.psum_scatter(-jnp.dot(full_vecs.T, weighted.T, precision=lax.Precisio...  30.8 us
    all_gather x1, waiting for transfers between devices, body(): full_rows = lax.all_gather(row_orbitals, 'cols', axis=1, tiled=True)  30.6 us
    dot_general x1, matrix products, body(): jnp.dot(full_rows, full_cols.T, precision=lax.Precision.HIGHEST, preferre...  7.69 us
    dot_general x1, matrix products, body(): jnp.dot(full_vecs.T, weighted.T, precision=lax.Precision.HIGHEST, preferr...  6.46 us
  transfers between devices with their start and end apart: 4, of which 4 were waited for; matrix products, arithmetic and copies ran while one was open for 2% of the time, Pallas kernels for 0%

profile of v1, /device:TPU:0, one launch (start us, length us, event | category | flops | bytes accessed | tf_op | source)
XLA Modules:
  0.0 181.3 jit_solution(101588713476415849)
XLA Ops:
  6.5 0.0 all-gather.9.cloned.1.call-start
  6.5 0.7 all-gather.9.cloned.1.call-update
  7.3 0.0 all-gather.5.cloned.1.call-start
  7.3 0.7 all-gather.5.cloned.1.call-update
  8.0 0.0 all-gather.7.cloned.1.call-start
  8.1 0.7 all-gather.7.cloned.1.call-update
  8.7 0.0 reduce-scatter.2.cloned.1.call-start
  8.8 43.2 %all-gather.9.cloned.1.call-done = f32[12288,32]{0,1:T(8,128)} async-done(((f32[768,32]{0,1:T(8,128)}), f32[12288,32]{0,1:T(8,128)}) %all-gather.9.cloned.1.call-update) | async-done | bytes 1572880 | tf_op jit(solution)/shard_map/all_gather | solution.py:10
  52.0 1.9 %copy.9 = f32[4,8,16,768]{3,2,1,0:T(8,128)S(1)} copy(f32[4,8,16,768]{3,1,2,0:T(8,128)} %bitcast.14) | data formatting | bytes 3145728
  53.9 0.9 copy.7
  54.8 30.6 %all-gather.5.cloned.1.call-done = f32[1024,512]{1,0:T(8,128)} async-done(((f32[1024,256]{1,0:T(8,128)}), f32[1024,512]{1,0:T(8,128)}) %all-gather.5.cloned.1.call-update) | async-done | bytes 2097168 | tf_op jit(solution)/shard_map/all_gather | solution.py:8
  85.4 41.9 %all-gather.7.cloned.1.call-done = f32[768,512]{0,1:T(8,128)} async-done(((f32[768,32]{0,1:T(8,128)}), f32[768,512]{0,1:T(8,128)}) %all-gather.7.cloned.1.call-update) | async-done | bytes 1572880 | tf_op jit(solution)/shard_map/all_gather | solution.py:9
  127.3 0.0 copy-start
  127.3 7.7 %fusion.4 = f32[1024,768]{1,0:T(8,128)S(1)} fusion(f32[1024,512]{1,0:T(8,128)} %all-gather.5.cloned.1.call-done, f32[768,512]{0,1:T(8,128)} %all-gather.7.cloned.1.call-done), kind=kOutput, calls=%fused_computation.3 | convolution fusion | flops 4831838208 | bytes 6815744 | tf_op jit(solution)/shard_map/dot_general | solution.py:11
  135.0 0.0 copy-done
  135.0 6.5 %negate_bitcast_fusion = f32[512,1024]{0,1:T(8,128)} fusion(f32[768,512]{0,1:T(8,128)S(1)} %bitcast.12, f32[1024,768]{1,0:T(8,128)S(1)} %copy-done, f32[1024,768]{1,0:T(8,128)S(1)} %fusion.4), kind=kOutput, calls=%fused_computation.2 | convolution fusion | flops 4833148928 | bytes 9961472 | tf_op jit(solution)/shard_map/dot_general | solution.py:16
  141.5 0.0 reduce-scatter.2.cloned.1.call-update
  141.5 30.8 %reduce-scatter.2.cloned.1.call-done = f32[256,1024]{0,1:T(8,128)} async-done(((f32[512,1024]{0,1:T(8,128)}), f32[256,1024]{0,1:T(8,128)}) %reduce-scatter.2.cloned.1.call-update) | async-done | bytes 1048592 | tf_op jit(solution)/shard_map/reduce_scatter | solution.py:15
  172.3 2.5 %copy.8 = f32[256,1024]{1,0:T(8,128)} copy(f32[256,1024]{0,1:T(8,128)} %reduce-scatter.2.cloned.1.call-done) | data formatting | bytes 2097152 | tf_op jit(solution)/shard_map/reduce_scatter | solution.py:15
Async XLA Ops:
  6.5 45.5 %all-gather.9.cloned.1.call-start = ((), (), s32[]{:S(2)}) async-start(), calls=%async_computation.4 | async-start | bytes 1671168 | tf_op jit(solution)/shard_map/all_gather | solution.py:10
  7.3 78.1 %all-gather.5.cloned.1.call-start = ((), (), s32[]{:S(2)}) async-start(), calls=%async_computation.1 | async-start | bytes 3145728 | tf_op jit(solution)/shard_map/all_gather | solution.py:8
  8.0 119.3 %all-gather.7.cloned.1.call-start = ((), (), s32[]{:S(2)}) async-start(), calls=%async_computation.2 | async-start | bytes 1671168 | tf_op jit(solution)/shard_map/all_gather | solution.py:9
  8.7 163.5 %reduce-scatter.2.cloned.1.call-start = ((), (), s32[]{:S(2)}) async-start(), calls=%async_computation.3 | async-start | bytes 3145728 | tf_op jit(solution)/shard_map/reduce_scatter | solution.py:15
  127.3 7.7 %copy-start = (f32[1024,768]{1,0:T(8,128)S(1)}, f32[1024,768]{1,0:T(8,128)}, u32[]{:S(2)}) copy-start(f32[1024,768]{1,0:T(8,128)} %param.4) | copy-start | bytes 9437188
Sparse Core Ops, SparseCore 0:
  9.6 42.3 all-gather.8
  53.5 31.8 all-gather.4
  87.7 39.5 all-gather.6
  141.6 30.6 reduce-scatter.1

commit v2 on v0

--- a/solution.py
+++ b/solution.py
@@ -6,8 +6,13 @@
 
 def body(kernel, row_orbitals, col_orbitals, col_vectors):
     full_rows = lax.all_gather(row_orbitals, "cols", axis=1, tiled=True)
-    full_cols = lax.all_gather(col_orbitals, "rows", axis=1, tiled=True)
-    full_vecs = lax.all_gather(col_vectors, "rows", axis=1, tiled=True)
+    full_cols, full_vecs = jnp.split(
+        lax.all_gather(
+            jnp.concatenate([col_orbitals, col_vectors], axis=0), "rows", axis=1, tiled=True
+        ),
+        [col_orbitals.shape[0]],
+        axis=0,
+    )
     gram = jnp.dot(
         full_rows, full_cols.T, precision=lax.Precision.HIGHEST, preferred_element_type=jnp.float32
     )

time: 176 us -> 144 us (0.82)
  waiting for transfers between devices: 144 us -> 115 us
  local copies, waits for them, and re-layouts: 2.53 us -> 0.01 us
    all_gather x2 -> x1, waiting for transfers between devices: 75.3 us -> 47.8 us  [body(): lax.all_gather(jnp.concatenate([col_orbitals, col_vectors], axis=0), 'row...]
    reduce_scatter x1 -> x0, local copies, waits for them, and re-layouts: 2.53 us -> none  [body(): lax.psum_scatter(-jnp.dot(full_vecs.T, weighted.T, precision=lax.Precisio...]
  transfers between devices with their start and end apart: 4 -> 3, of which waited for: 4 -> 3; matrix products, arithmetic and copies ran while one was open for 4% -> 1% of each run, Pallas kernels for 0% -> 0%
where the time goes in v2:
time: 144 us
  waiting for transfers between devices  115 us (80%)
  matrix products  14.5 us (10%)
  between operations  13.1 us (9%)
  other arithmetic  1.63 us (1%)
    all_gather x1, waiting for transfers between devices, body(): lax.all_gather(jnp.concatenate([col_orbitals, col_vectors], axis=0), 'row...  47.8 us
    all_gather x1, waiting for transfers between devices, body(): full_rows = lax.all_gather(row_orbitals, 'cols', axis=1, tiled=True)  35.7 us
    reduce_scatter x1, waiting for transfers between devices, body(): lax.psum_scatter(-jnp.dot(full_vecs.T, weighted.T, precision=lax.Precisio...  30.4 us
    dot_general x1, matrix products, body(): jnp.dot(full_rows, full_cols.T, precision=lax.Precision.HIGHEST, preferre...  7.89 us
    dot_general x1, matrix products, body(): jnp.dot(full_vecs.T, weighted.T, precision=lax.Precision.HIGHEST, preferr...  6.63 us
  transfers between devices with their start and end apart: 3, of which 3 were waited for; matrix products, arithmetic and copies ran while one was open for 1% of the time, Pallas kernels for 0%

profile of v2, /device:TPU:0, one launch (start us, length us, event | category | flops | bytes accessed | tf_op | source)
XLA Modules:
  0.0 144.0 jit_solution(4368060337229305844)
XLA Ops:
  6.5 0.0 all-gather.5.cloned.1.call-start
  6.5 0.7 all-gather.5.cloned.1.call-update
  7.3 0.0 all-gather.3.cloned.1.call-start
  7.3 1.6 %pad_maximum_fusion = f32[1536,32]{0,1:T(8,128)} fusion(f32[768,32]{0,1:T(8,128)} %param.7, f32[768,32]{0,1:T(8,128)} %param.6), kind=kLoop, calls=%fused_computation.6 | loop fusion | flops 49152 | bytes 393216 | tf_op jit(solution)/shard_map/concatenate | solution.py:11
  8.9 0.0 all-gather.3.cloned.1.call-update
  9.0 0.0 copy-start.1
  9.0 0.0 reduce-scatter.2.cloned.1.call-start
  9.0 35.7 %all-gather.5.cloned.1.call-done = f32[1024,512]{1,0:T(8,128)} async-done(((f32[1024,256]{1,0:T(8,128)}), f32[1024,512]{1,0:T(8,128)}) %all-gather.5.cloned.1.call-update) | async-done | bytes 2097168 | tf_op jit(solution)/shard_map/all_gather | solution.py:8
  44.7 47.8 %all-gather.3.cloned.1.call-done = f32[1536,512]{0,1:T(8,128)} async-done(((f32[1536,32]{0,1:T(8,128)}), f32[1536,512]{0,1:T(8,128)}) %all-gather.3.cloned.1.call-update) | async-done | bytes 3145744 | tf_op jit(solution)/shard_map/all_gather | solution.py:10
  92.5 0.0 copy-start
  92.5 7.9 %fusion.2 = f32[768,1024]{0,1:T(8,128)S(1)} fusion(f32[1024,512]{1,0:T(8,128)} %all-gather.5.cloned.1.call-done, f32[1536,512]{0,1:T(8,128)} %all-gather.3.cloned.1.call-done), kind=kOutput, calls=%fused_computation.3 | convolution fusion | flops 4831838208 | bytes 6815744 | tf_op jit(solution)/shard_map/dot_general | solution.py:16
  100.4 0.0 copy-done.1
  100.4 0.0 copy-done
  100.4 6.6 %fusion.1 = f32[512,1024]{1,0:T(8,128)} fusion(f32[1024,768]{1,0:T(8,128)S(1)} %copy-done.1, f32[768,1024]{0,1:T(8,128)S(1)} %fusion.2, f32[1536,512]{0,1:T(8,128)S(1)} %copy-done), kind=kOutput, calls=%fused_computation.2 | convolution fusion | flops 4833148928 | bytes 9961472 | tf_op jit(solution)/shard_map/dot_general | solution.py:21
  107.0 0.0 reduce-scatter.2.cloned.1.call-update
  107.1 30.4 %reduce-scatter.2.cloned.1.call-done = f32[256,1024]{1,0:T(8,128)} async-done(((f32[512,1024]{1,0:T(8,128)}), f32[256,1024]{1,0:T(8,128)}) %reduce-scatter.2.cloned.1.call-update) | async-done | bytes 1048592 | tf_op jit(solution)/shard_map/reduce_scatter | solution.py:20
Async XLA Ops:
  6.5 38.2 %all-gather.5.cloned.1.call-start = ((), (), s32[]{:S(2)}) async-start(), calls=%async_computation.2 | async-start | bytes 3145728 | tf_op jit(solution)/shard_map/all_gather | solution.py:8
  7.3 85.2 %all-gather.3.cloned.1.call-start = ((), (), s32[]{:S(2)}) async-start(), calls=%async_computation.1 | async-start | bytes 3342336 | tf_op jit(solution)/shard_map/all_gather | solution.py:10
  9.0 91.4 %copy-start.1 = (f32[1024,768]{1,0:T(8,128)S(1)}, f32[1024,768]{1,0:T(8,128)}, u32[]{:S(2)}) copy-start(f32[1024,768]{1,0:T(8,128)} %param.4) | copy-start | bytes 9437188
  9.0 128.5 %reduce-scatter.2.cloned.1.call-start = ((), (), s32[]{:S(2)}) async-start(), calls=%async_computation.3 | async-start | bytes 3145728 | tf_op jit(solution)/shard_map/reduce_scatter | solution.py:20
  92.5 7.9 %copy-start = (f32[1536,512]{0,1:T(8,128)S(1)}, f32[1536,512]{0,1:T(8,128)}, u32[]{:S(2)}) copy-start(f32[1536,512]{0,1:T(8,128)} %all-gather.3.cloned.1.call-done) | copy-start | bytes 9437188
Sparse Core Ops, SparseCore 0:
  8.9 35.8 all-gather.4
  47.0 45.4 all-gather.2
  107.2 30.2 reduce-scatter.1
